TPU v7x, 128 devices: a whole 4x4x4 slice. The times are simulated.
128 devices in a mesh: node: 8 (over y_lo, z), bond: 16 (over y_hi, x, core).
Axes of the slice: x: 4, y: 4 (y_hi: 2, y_lo: 2; y = y_hi * 2 + y_lo), z: 4, core: 2. Of those that a mesh axis runs over, the one named last changes fastest.
Arguments:
- bottom_nodes: float32 [8, 128, 128, 128], P('node', 'bond'), may hold values from -0.046875 to 0.046875
- upper_nodes: float32 [8, 128, 128, 128], P(None, 'bond', 'node'), may hold values from -0.046875 to 0.046875
- leaf_up: float32 [8, 3, 2, 128, 128], P('node'), may hold values from -2 to 3
- outside_env: float32 [3, 128, 128], replicated, may hold values from -2 to 3
- top_env: float32 [3, 128, 128], replicated, may hold values from -2 to 3
Outputs:
- leaf_down: float32 [8, 3, 2, 128, 128], P('node', None, None, 'bond')
- subtree_env: float32 [3, 128, 128], replicated
All inputs are finite; a program needn't handle non-finite values.
Results may differ from a plain program's by a relative error of at most 0.0001.
Values sent between devices are 32-bit elements; how exact they have to be, the bound alone decides.
No kernel may reach another device: no remote copies, remote signals or barrier semaphores. Data moves between devices by JAX's collectives and lax.ppermute only.
A program may use at most 128 MiB of HBM per device.

v0:
```python
import jax
import jax.numpy as jnp
from jax import lax
from jax.sharding import PartitionSpec as P

highest = lax.Precision.HIGHEST


def from_everyone(x, axis):
    copies = jnp.broadcast_to(x, (lax.axis_size(axis), *x.shape))
    return lax.all_to_all(copies, axis, split_axis=0, concat_axis=0, tiled=True)


def over_copies(x, axis):
    return from_everyone(x, axis).sum(axis=0)


def in_order(pieces, dim):
    dims = list(pieces.shape[1:])
    dims[dim] *= pieces.shape[0]
    return jnp.moveaxis(pieces, 0, dim).reshape(dims)


def gather_directly(x, axis, dim):
    return in_order(from_everyone(x, axis), dim)


def packed_total(arrays, axis):
    ends = [0]
    for a in arrays:
        ends.append(ends[-1] + a.size)
    running = lax.psum(jnp.concatenate([a.ravel() for a in arrays]), axis)
    return tuple((running[b:e].reshape(a.shape) for a, b, e in zip(arrays, ends, ends[1:])))


def in_blocks(x, dim, length):
    before, after = (x.shape[:dim], x.shape[dim + 1 :])
    return jnp.moveaxis(x.reshape(*before, length, -1, *after), dim, 0)


def summed_on_arrival(x, axis, dim):
    length = lax.axis_size(axis)
    pieces = lax.all_to_all(in_blocks(x, dim, length), axis, 0, 0, tiled=True)
    return jnp.sum(pieces, axis=0)


def side_by_side(arrays, axis, dim, along):
    both = jnp.concatenate(arrays, axis=along)
    filled, at, finished = (summed_on_arrival(both, axis, dim), 0, [])
    for a in arrays:
        finished.append(lax.slice_in_dim(filled, at, at + a.shape[along], axis=along))
        at += a.shape[along]
    return tuple(finished)


def grow_product(tensor, left_env, right_env):
    middle = jnp.einsum("skac,spcd->skpad", left_env, tensor, precision=highest)
    return jnp.einsum("skpad,skbd->skpab", middle, right_env, precision=highest)


def gram_partial(tensor, product):
    return jnp.einsum("spab,skqab->skpq", tensor, product, precision=highest)


def first_part(tensor, worked, right_env):
    first = jnp.einsum("skpcd,skbd->skpcb", worked, right_env, precision=highest)
    return jnp.einsum("spab,skpcb->skac", tensor, first, precision=highest)


def second_part(tensor, worked, left_env):
    second = jnp.einsum("skac,skpcd->skpad", left_env, worked, precision=highest)
    return jnp.einsum("spab,skpad->skbd", tensor, second, precision=highest)


def upper_up(columns, parents, left_env, right_env):
    middle = jnp.einsum("skac,spcd->skpad", left_env, columns, precision=highest)
    middle_rows = lax.all_to_all(middle, "node", split_axis=3, concat_axis=4, tiled=True)
    product = jnp.einsum("skpad,skbd->skpab", middle_rows, right_env, precision=highest)
    product_all = lax.all_to_all(product, "bond", split_axis=4, concat_axis=2, tiled=True)
    return lax.psum(gram_partial(parents, product_all), ("node", "bond"))


def down_parts(columns, parents, above, left_env, right_env, with_second):
    worked_all = jnp.einsum("skpq,sqcd->skpcd", above, parents, precision=highest)
    worked = lax.all_to_all(worked_all, "bond", split_axis=2, concat_axis=4, tiled=True)
    first_rows = jnp.einsum("skpcd,skbd->skpcb", worked, right_env, precision=highest)
    first_cols = lax.all_to_all(first_rows, "node", split_axis=4, concat_axis=3, tiled=True)
    first_env = jnp.einsum("spab,skpcb->skac", columns, first_cols, precision=highest)
    if not with_second:
        return (first_env,)
    side = jnp.einsum("spab,skac->skpcb", columns, left_env, precision=highest)
    side_rows = lax.all_to_all(side, "node", split_axis=3, concat_axis=4, tiled=True)
    second_env = jnp.einsum("skpcb,skpcd->skbd", side_rows, worked, precision=highest)
    return (first_env, second_env)


def local(bottom_nodes, upper_nodes, leaf_up, outside_env, top_env):
    nodes = lax.axis_size("node")
    width = bottom_nodes.shape[2]
    rows = bottom_nodes.shape[1]
    operators = leaf_up.shape[1]
    left_leaf = leaf_up[:, :, 0]
    right_leaf = leaf_up[:, :, 1]
    product = grow_product(bottom_nodes, left_leaf, right_leaf)
    tensor_a = lax.all_to_all(bottom_nodes, "bond", split_axis=2, concat_axis=1, tiled=True)
    product_a = lax.all_to_all(product, "bond", split_axis=3, concat_axis=2, tiled=True)
    own_env = over_copies(gram_partial(tensor_a, product_a), "bond")
    children = gather_directly(own_env, "node", 0)
    upper_cols = lax.all_to_all(upper_nodes, "node", split_axis=3, concat_axis=2, tiled=True)
    upper_pars = lax.all_to_all(upper_nodes, "bond", split_axis=3, concat_axis=1, tiled=True)
    ups = {nodes: children}
    level_size = nodes // 2
    while level_size >= 1:
        below = ups[2 * level_size]
        ups[level_size] = upper_up(
            upper_cols[level_size : 2 * level_size],
            upper_pars[level_size : 2 * level_size],
            below[0::2],
            below[1::2],
        )
        level_size = level_size // 2
    root_env = ups[1]
    crown_part = down_parts(
        upper_cols[0:1], upper_pars[0:1], top_env[None], root_env, outside_env[None], False
    )[0]
    above = lax.psum(crown_part, ("node", "bond"))
    level_size = 1
    while level_size < nodes:
        below = ups[2 * level_size]
        first_env, second_env = down_parts(
            upper_cols[level_size : 2 * level_size],
            upper_pars[level_size : 2 * level_size],
            above,
            below[0::2],
            below[1::2],
            True,
        )
        first_env, second_env = packed_total((first_env, second_env), ("node", "bond"))
        above = jnp.stack([first_env, second_env], 1).reshape(
            2 * level_size, operators, width, width
        )
        level_size = level_size * 2
    mine = lax.dynamic_index_in_dim(above, lax.axis_index("node"), 0, keepdims=True)
    own_rows = lax.dynamic_slice_in_dim(mine, lax.axis_index("bond") * rows, rows, 2)
    worked = jnp.einsum(
        "skpq,sqcd->skpcd",
        own_rows,
        lax.all_gather(bottom_nodes, "bond", axis=1, tiled=True),
        precision=highest,
    )
    first_env = first_part(bottom_nodes, worked, right_leaf)
    second_env = second_part(bottom_nodes, worked, left_leaf)
    first_env, second_env = side_by_side((first_env, second_env), "bond", 2, 0)
    leaf_down = jnp.stack([first_env, second_env], 2)
    return (leaf_down, root_env[0])


def solution(mesh):
    placed = (
        P("node", "bond", None, None),
        P(None, "bond", "node", None),
        P("node", None, None, None, None),
        P(),
        P(),
    )
    return jax.shard_map(
        local,
        mesh=mesh,
        in_specs=placed,
        out_specs=(P("node", None, None, "bond", None), P()),
        check_vma=False,
    )
```

profile of v0, /device:TPU:1, one launch (start us, length us, event | category | flops | bytes accessed | tf_op | source)
XLA Modules:
  0.0 1421.0 jit_solution(13063152270408654019)
XLA Ops:
  10.3 8.4 all-to-all-start.6
  29.7 26.2 %all_to_all.360 = f32[1,3,8,128,128]{4,2,1,0,3:T(8,128)S(1)} all-to-all(f32[1,3,8,128,128]{4,2,1,0,3:T(8,128)S(1)} %copy.237), channel_id=1, replica_groups=mesh['node'=8,'bond'=16] {'bond'}, dimensions={3} | all-to-all | bytes 3145728 | tf_op jit(solution)/shard_map/all_to_all | solution.py:106
  74.2 31.9 %all-to-all-done.7 = f32[16,1,3,128,128]{4,3,2,1,0:T(8,128)S(1)} async-done(((f32[16,1,3,128,128]{4,3,2,1,0:T(8,128)}), f32[16,1,3,128,128]{4,3,2,1,0:T(8,128)S(1)}, u32[]{:S(2)}, u32[]{:S(2)}) %all-to-all-start.7) | async-done | bytes 3145760 | tf_op jit(solution)/shard_map/all_to_all | solution.py:11
  111.4 7.7 all-to-all-done.3
  166.7 7.5 all-to-all-done.9
  174.3 7.8 all-to-all-start
  189.3 9.0 copy.468
  215.9 7.2 all-to-all-start.10
  250.3 6.7 fusion.39
  263.2 6.8 all-to-all-start.1
  270.0 134.2 %all-reduce.8.cloned.1.call-done = f32[4,3,128,128]{2,3,1,0:T(8,128)} async-done(((f32[4,3,128,128]{2,3,1,0:T(8,128)}), f32[4,3,128,128]{2,3,1,0:T(8,128)}) %all-reduce.8.cloned.1.call-update) | async-done | bytes 786448 | tf_op jit(solution)/shard_map/psum | solution.py:80
  470.1 147.5 %all-reduce.16.cloned.1.call-done = (f32[2,3,128,128]{2,3,1,0:T(8,128)}, f32[3,128,128]{1,2,0:T(8,128)}) async-done(((f32[2,3,128,128]{2,3,1,0:T(8,128)}, f32[3,128,128]{1,2,0:T(8,128)}), (f32[2,3,128,128]{2,3,1,0:T(8,128)}, f32[3,128,128]{1,2,0:T(8,128)})) %all-reduce.16.cloned.1.call-update) | async-done | bytes 589840 | tf_op jit(solution)/shard_map/psum | solution.py:80
  630.7 6.9 all-to-all-start.4
  669.1 142.6 %all-reduce.10.cloned.1.call-done = f32[98304]{0:T(1024)} async-done(((f32[98304]{0:T(1024)}), f32[98304]{0:T(1024)}) %all-reduce.10.cloned.1.call-update) | async-done | bytes 393232 | tf_op jit(solution)/shard_map/psum | solution.py:32
  843.7 6.8 fusion.12
  877.8 6.9 fusion.10
  905.6 139.7 %all-reduce.12.cloned.1.call-done = f32[196608]{0:T(1024)} async-done(((f32[196608]{0:T(1024)}), f32[196608]{0:T(1024)}) %all-reduce.12.cloned.1.call-update) | async-done | bytes 786448 | tf_op jit(solution)/shard_map/psum | solution.py:32
  1105.5 11.9 fusion.4
  1142.4 9.0 copy.466
  1161.1 12.4 fusion.2
  1180.7 9.0 copy.467
  1199.3 178.5 %all-reduce.14.cloned.1.call-done = (f32[393216]{0:T(1024)}, f32[3,128,128]{1,2,0:T(8,128)}) async-done(((f32[393216]{0:T(1024)}, f32[3,128,128]{1,2,0:T(8,128)}), (f32[393216]{0:T(1024)}, f32[3,128,128]{1,2,0:T(8,128)})) %all-reduce.14.cloned.1.call-update) | async-done | bytes 1769488 | tf_op jit(solution)/shard_map/psum | solution.py:32
  1379.5 7.5 fusion
  1404.1 8.9 all-to-all-done.21
  (284 shorter events, 463.3 us)
Async XLA Ops:
  10.3 19.4 %all-to-all-start.6 = ((f32[1,8,128,128]{3,1,0,2:T(8,128)}), f32[1,8,128,128]{3,1,0,2:T(8,128)S(1)}, u32[]{:S(2)}, u32[]{:S(2)}) async-start(f32[1,8,128,128]{3,1,0,2:T(8,128)} %copy.239), calls=%async_computation.6 | async-start | bytes 1048576 | tf_op jit(solution)/shard_map/all_to_all | solution.py:105
  59.5 46.6 %all-to-all-start.7 = ((f32[16,1,3,128,128]{4,3,2,1,0:T(8,128)}), f32[16,1,3,128,128]{4,3,2,1,0:T(8,128)S(1)}, u32[]{:S(2)}, u32[]{:S(2)}) async-start(f32[16,1,3,128,128]{4,3,2,1,0:T(8,128)} %broadcast_in_dim.8), calls=%async_computation.7 | async-start | bytes 6291456 | tf_op jit(solution)/shard_map/all_to_all | solution.py:11
  120.5 26.0 %all-to-all-start.8 = ((f32[8,1,3,128,128]{4,3,2,1,0:T(8,128)}), f32[8,1,3,128,128]{4,3,2,1,0:T(8,128)S(1)}, u32[]{:S(2)}, u32[]{:S(2)}) async-start(f32[8,1,3,128,128]{4,3,2,1,0:T(8,128)} %broadcast_in_dim.9), calls=%async_computation.8 | async-start | bytes 3145728 | tf_op jit(solution)/shard_map/all_to_all | solution.py:11
  158.9 15.3 %all-to-all-start.9 = ((f32[8,1,24576]{2,1,0:T(1,128)}), f32[8,1,24576]{2,1,0:T(1,128)S(1)}, u32[]{:S(2)}, u32[]{:S(2)}) async-start(f32[8,1,24576]{2,1,0:T(1,128)} %reshape.318), calls=%async_computation.9 | async-start | bytes 1572864 | tf_op jit(solution)/shard_map/all_to_all | solution.py:77
  174.3 41.6 %all-to-all-start = ((f32[16,1,8192]{2,1,0:T(1,128)}), f32[16,1,8192]{2,1,0:T(1,128)}, u32[]{:S(2)}, u32[]{:S(2)}) async-start(f32[16,1,8192]{2,1,0:T(1,128)} %reshape.316), calls=%async_computation | async-start | bytes 1048576 | tf_op jit(solution)/shard_map/all_to_all | solution.py:110
  215.9 21.5 %all-to-all-start.10 = ((f32[16,1,12288]{2,1,0:T(1,128)}), f32[16,1,12288]{2,1,0:T(1,128)S(1)}, u32[]{:S(2)}, u32[]{:S(2)}) async-start(f32[16,1,12288]{2,1,0:T(1,128)} %reshape.320), calls=%async_computation.10 | async-start | bytes 1572864 | tf_op jit(solution)/shard_map/all_to_all | solution.py:79
  223.1 181.1 %all-reduce.8.cloned.1.call-start = ((), (), s32[]{:S(2)}) async-start(), calls=%async_computation.24 | async-start | bytes 1572864 | tf_op jit(solution)/shard_map/psum | solution.py:80
  263.2 147.2 %all-to-all-start.1 = ((f32[16,1,3072]{2,1,0:T(1,128)}), f32[16,1,3072]{2,1,0:T(1,128)S(1)}, u32[]{:S(2)}, u32[]{:S(2)}) async-start(f32[16,1,3072]{2,1,0:T(1,128)} %reshape.330), calls=%async_computation.1 | async-start | bytes 393216 | tf_op jit(solution)/shard_map/all_to_all | solution.py:85
  423.0 20.8 %all-to-all-start.2 = ((f32[8,1,6144]{2,1,0:T(1,128)}), f32[8,1,6144]{2,1,0:T(1,128)S(1)}, u32[]{:S(2)}, u32[]{:S(2)}) async-start(f32[8,1,6144]{2,1,0:T(1,128)} %reshape.332), calls=%async_computation.2 | async-start | bytes 393216 | tf_op jit(solution)/shard_map/all_to_all | solution.py:87
  443.8 15.9 %all-to-all-start.12 = ((f32[16,1,6144]{2,1,0:T(1,128)}), f32[16,1,6144]{2,1,0:T(1,128)}, u32[]{:S(2)}, u32[]{:S(2)}) async-start(f32[16,1,6144]{2,1,0:T(1,128)} %reshape.326), calls=%async_computation.12 | async-start | bytes 786432 | tf_op jit(solution)/shard_map/all_to_all | solution.py:79
  450.0 167.6 %all-reduce.16.cloned.1.call-start = ((), (), s32[]{:S(2)}) async-start(), calls=%async_computation.29 | async-start | bytes 1179648 | tf_op jit(solution)/shard_map/psum | solution.py:80
  658.8 152.9 %all-reduce.10.cloned.1.call-start = ((), (), s32[]{:S(2)}) async-start(), calls=%async_computation.25 | async-start | bytes 786432 | tf_op jit(solution)/shard_map/psum | solution.py:32
  818.0 15.9 %all-to-all-start.15 = ((f32[16,1,6144]{2,1,0:T(1,128)}), f32[16,1,6144]{2,1,0:T(1,128)}, u32[]{:S(2)}, u32[]{:S(2)}) async-start(f32[16,1,6144]{2,1,0:T(1,128)} %reshape.338), calls=%async_computation.15 | async-start | bytes 786432 | tf_op jit(solution)/shard_map/all_to_all | solution.py:85
  834.0 23.0 %all-to-all-start.17 = ((f32[8,1,12288]{2,1,0:T(1,128)}), f32[8,1,12288]{2,1,0:T(1,128)}, u32[]{:S(2)}, u32[]{:S(2)}) async-start(f32[8,1,12288]{2,1,0:T(1,128)} %reshape.322), calls=%async_computation.17 | async-start | bytes 786432 | tf_op jit(solution)/shard_map/all_to_all | solution.py:92
  857.0 27.7 %all-to-all-start.16 = ((f32[8,1,12288]{2,1,0:T(1,128)}), f32[8,1,12288]{2,1,0:T(1,128)}, u32[]{:S(2)}, u32[]{:S(2)}) async-start(f32[8,1,12288]{2,1,0:T(1,128)} %reshape.340), calls=%async_computation.16 | async-start | bytes 786432 | tf_op jit(solution)/shard_map/all_to_all | solution.py:87
  862.1 183.2 %all-reduce.12.cloned.1.call-start = ((), (), s32[]{:S(2)}) async-start(), calls=%async_computation.26 | async-start | bytes 1572864 | tf_op jit(solution)/shard_map/psum | solution.py:32
  900.5 158.6 %all-to-all-start.22 = ((f32[8,1,6144]{2,1,0:T(1,128)}), f32[8,1,6144]{2,1,0:T(1,128)S(1)}, u32[]{:S(2)}, u32[]{:S(2)}) async-start(f32[8,1,6144]{2,1,0:T(1,128)} %reshape.346), calls=%async_computation.22 | async-start | bytes 393216 | tf_op jit(solution)/shard_map/all_to_all | solution.py:77
  1059.1 20.6 %all-to-all-start.18 = ((f32[16,1,12288]{2,1,0:T(1,128)}), f32[16,1,12288]{2,1,0:T(1,128)S(1)}, u32[]{:S(2)}, u32[]{:S(2)}) async-start(f32[16,1,12288]{2,1,0:T(1,128)} %reshape.342), calls=%async_computation.18 | async-start | bytes 1572864 | tf_op jit(solution)/shard_map/all_to_all | solution.py:85
  1079.6 19.7 %all-to-all-start.20 = ((f32[8,1,24576]{2,1,0:T(1,128)}), f32[8,1,24576]{2,1,0:T(1,128)}, u32[]{:S(2)}, u32[]{:S(2)}) async-start(f32[8,1,24576]{2,1,0:T(1,128)} %reshape.314), calls=%async_computation.20 | async-start | bytes 1572864 | tf_op jit(solution)/shard_map/all_to_all | solution.py:92
  1099.3 29.6 %all-to-all-start.23 = ((f32[16,1,3072]{2,1,0:T(1,128)}), f32[16,1,3072]{2,1,0:T(1,128)S(1)}, u32[]{:S(2)}, u32[]{:S(2)}) async-start(f32[16,1,3072]{2,1,0:T(1,128)} %reshape.348), calls=%async_computation.23 | async-start | bytes 393216 | tf_op jit(solution)/shard_map/all_to_all | solution.py:79
  1129.0 44.5 %all-to-all-start.19 = ((f32[8,1,24576]{2,1,0:T(1,128)}), f32[8,1,24576]{2,1,0:T(1,128)S(1)}, u32[]{:S(2)}, u32[]{:S(2)}) async-start(f32[8,1,24576]{2,1,0:T(1,128)} %reshape.344), calls=%async_computation.19 | async-start | bytes 1572864 | tf_op jit(solution)/shard_map/all_to_all | solution.py:87
  1133.8 244.0 %all-reduce.14.cloned.1.call-start = ((), (), s32[]{:S(2)}) async-start(), calls=%async_computation.28 | async-start | bytes 3538944 | tf_op jit(solution)/shard_map/psum | solution.py:32
  1197.1 182.3 %all-gather.2.cloned.1.call-start = ((), (), s32[]{:S(2)}) async-start(), calls=%async_computation.27 | async-start | bytes 8912896 | tf_op jit(solution)/shard_map/all_gather | solution.py:148
  1397.0 15.9 %all-to-all-start.21 = ((f32[16,2,3,8,128]{4,3,2,1,0:T(8,128)}), f32[16,2,3,8,128]{4,3,2,1,0:T(8,128)S(1)}, u32[]{:S(2)}, u32[]{:S(2)}) async-start(f32[16,2,3,8,128]{4,3,2,1,0:T(8,128)} %copy_bitcast_fusion.13), calls=%async_computation.21 | async-start | bytes 786432 | tf_op jit(solution)/shard_map/all_to_all | solution.py:43
  (36 other events, 643.5 us)
Sparse Core Ops, SparseCore 0:
  257.1 147.0 all-reduce.7
  470.0 147.5 all-reduce.15
  669.2 142.3 all-reduce.9
  898.5 146.7 all-reduce.11
  1197.2 180.5 all-reduce.13
Sparse Core Ops, SparseCore 1:
  1199.9 81.7 all-gather.1
where the time goes:
time: 1430 us; the launch traced here: 1420 us
  waiting for transfers between devices  823 us (58%)
  local copies, waits for them, and re-layouts  275 us (19%)
  starting transfers between devices  129 us (9%)
  matrix products  101 us (7%)
  other arithmetic  50.9 us (4%)
  blocking collectives  26.2 us (2%)
  between operations  16.5 us (1%)
    psum x3, waiting for transfers between devices, packed_total(): running = lax.psum(jnp.concatenate([a.ravel() for a in arrays]), axis)  461 us
    psum x2, waiting for transfers between devices, upper_up(): return lax.psum(gram_partial(parents, product_all), ('node', 'bond'))  282 us
    unnamed x104, local copies, waits for them, and re-layouts  117 us
    all_to_all x2, waiting for transfers between devices, from_everyone(): return lax.all_to_all(copies, axis, split_axis=0, concat_axis=0, tiled=True)  35.4 us
  transfers between devices with their start and end apart: 29, of which 18 were waited for; matrix products, arithmetic and copies ran while one was open for 19% of the time, Pallas kernels for 0%

commit v1 on v0

v1 whole, which is shorter than its diff:
```python
import jax
import jax.numpy as jnp
from jax import lax
from jax.sharding import Mesh, PartitionSpec as P

NODE = ("ylo", "zhi", "zlo")
BOND = ("yhi", "x", "core")
SLOT_OF = (4, 2, 5, 1, 6, 3, 7, 0)


def ein(spec, a, b):
    return jnp.einsum(spec, a, b, precision=lax.Precision.HIGHEST)


def after(x, other):
    return lax.optimization_barrier((x, other))[0]


def swap_cores(half, core, axis):
    other = lax.ppermute(half, "core", [(0, 1), (1, 0)])
    low = jnp.where(core == 0, half, other)
    high = jnp.where(core == 0, other, half)
    return jnp.concatenate([low, high], axis=axis)


def up_rows(tensor, rows, left_env, right_env):
    middle = ein("pab,ac->pcb", rows, left_env)
    product = ein("pcb,bd->pcd", middle, right_env)
    return ein("pcd,qcd->pq", product, tensor)


def halves(tensor, core, axis):
    size = tensor.shape[axis] // 2
    return lax.dynamic_slice_in_dim(tensor, core * size, size, axis=axis)


def local(bottom_nodes, upper_nodes, leaf_up, outside_env, top_env):
    group = lax.axis_index(NODE)
    bond = lax.axis_index(BOND)
    core = lax.axis_index("core")
    op = jnp.minimum(lax.axis_index("x"), 2)
    width = bottom_nodes.shape[2]
    rows = bottom_nodes.shape[1]
    parts = width // rows

    send = jnp.stack([upper_nodes[s] for s in SLOT_OF])
    got = lax.all_to_all(send, NODE, 0, 0, tiled=True)
    shard = jnp.moveaxis(got, 0, 1).reshape(rows, width, width)
    upper = lax.all_gather(shard, BOND, axis=0, tiled=True)

    mine = bottom_nodes[0]
    left_leaf = leaf_up[0, :, 0]
    right_leaf = leaf_up[0, :, 1]
    middle = ein("kac,pcd->kpad", left_leaf, after(mine, shard))
    product = ein("kpad,kbd->kpab", middle, right_leaf)
    both = jnp.concatenate([mine[None], product])
    both = jnp.moveaxis(both.reshape(4, rows, parts, rows, width), 2, 0)
    both = lax.all_to_all(both, BOND, 0, 0, tiled=True)
    both = jnp.moveaxis(both, 1, 0).reshape(4, width, rows, width)
    mine_a = both[0]
    gram = ein("pab,kqab->kpq", mine_a, both[1:])
    pieces = jnp.moveaxis(gram.reshape(3, parts, rows, width), 1, 0)
    pieces = lax.all_to_all(pieces, BOND, 0, 0, tiled=True)
    env = jnp.sum(pieces, axis=0)
    by_x = jnp.stack([env[0], env[1], env[2], env[2]])
    by_dest = jnp.broadcast_to(by_x[None, None, :, None], (2, 2, 4, 2, rows, width))
    by_dest = by_dest.reshape(2 * parts, rows, width)
    pair = lax.all_to_all(by_dest, ("zlo",) + BOND, 0, 0, tiled=True)
    left3, right3 = pair.reshape(2, width, width)

    def move(x, *pairs):
        return lax.ppermute(x, NODE, pairs)

    upper_rows = halves(upper, core, 0)
    up2 = up_rows(upper, upper_rows, left3, right3)
    ends = jnp.stack([move(up2, (0, 1), (4, 5)), move(up2, (2, 1), (6, 5))])
    left2, right2 = swap_cores(ends, core, 1)
    up1 = up_rows(upper, upper_rows, left2, right2)
    ends = jnp.stack([move(up1, (1, 3)), move(up1, (5, 3))])
    left1, right1 = swap_cores(ends, core, 1)

    upper_a = halves(upper, core, 1)
    upper_b = halves(upper, core, 2)

    def first_row(right_env):
        return ein("pab,bd->pad", upper_a, right_env)

    def second_row(left_env):
        return ein("pab,ac->pcb", upper_b, left_env)

    def worked_by(above):
        return ein("pq,qcd->pcd", above, upper)

    def first_of(row, worked):
        return ein("pad,pcd->ac", row, worked)

    def second_of(row, worked):
        return ein("pcb,pcd->bd", row, worked)

    top = lax.dynamic_index_in_dim(top_env, op, 0, keepdims=False)
    outside = lax.dynamic_index_in_dim(outside_env, op, 0, keepdims=False)
    crown = first_of(first_row(outside), worked_by(top))
    above = swap_cores(move(crown, (7, 3)), core, 0)
    worked = worked_by(above)
    first = first_of(first_row(right1), worked)
    second = second_of(second_row(left1), worked)
    root = up_rows(upper, upper_rows, left1, right1)
    above = swap_cores(move(first, (3, 1)) + move(second, (3, 5)), core, 0)
    worked = worked_by(above)
    first = first_of(first_row(right2), worked)
    second = second_of(second_row(left2), worked)
    above = move(first, (1, 0), (5, 4)) + move(second, (1, 2), (5, 6))
    above = swap_cores(above, core, 0)
    worked = worked_by(above)
    first = first_of(first_row(right3), worked)
    second = second_of(second_row(left3), worked)
    sent = move(second, (0, 1), (2, 3), (4, 5), (6, 7))
    last = jnp.where(group % 2 == 0, first, sent)

    root = jnp.where(group == 3, root, 0.0)
    root = root + move(root, (3, 7))
    root = root + move(root, (3, 1), (7, 5))
    root = root + move(root, (3, 2), (1, 0), (7, 6), (5, 4))
    ends = lax.all_gather(jnp.stack([last, root]), "x", axis=0, tiled=False)
    ends = swap_cores(ends[:3], core, 2)
    above = ends[:, 0]
    root_env = ends[:, 1]

    whole = lax.all_gather(after(mine, upper), BOND, axis=0, tiled=True)
    row = ein("pab,kbd->kpad", mine_a, right_leaf)
    grown = ein("kpq,kpad->kqad", above, row)
    first = ein("kqad,qcd->kac", grown, whole)
    turned = lax.dynamic_slice_in_dim(jnp.swapaxes(whole, 1, 2), bond * rows, rows, axis=1)
    row = ein("pba,kac->kbpc", turned, left_leaf)
    grown = ein("kpq,kbpc->kbqc", above, row)
    second = ein("kbqc,qcd->kbd", grown, whole)
    leaf_down = jnp.stack([first, second], 1)[None]
    return leaf_down, root_env


def solution(mesh):
    shape = (2, 2, 2, 2, 4, 2)
    fine = Mesh(mesh.devices.reshape(shape), NODE + BOND)
    placed = (
        P(NODE, BOND, None, None),
        P(None, BOND, NODE, None),
        P(NODE, None, None, None, None),
        P(),
        P(),
    )
    return jax.shard_map(
        local,
        mesh=fine,
        in_specs=placed,
        out_specs=(P(NODE, None, None, BOND, None), P()),
        check_vma=False,
    )
```

time: 1430 us -> 516 us (0.36)
  waiting for transfers between devices: 823 us -> 43.7 us
  local copies, waits for them, and re-layouts: 275 us -> 108 us
  matrix products: 101 us -> 236 us
  starting transfers between devices: 129 us -> 32.5 us
  other arithmetic: 50.9 us -> 1.12 us
  blocking collectives: 26.2 us -> 68.9 us
    psum x5 -> x0, waiting for transfers between devices: 743 us -> none  [the longest x3 461 us: packed_total(): running = lax.psum(jnp.concatenate([a.ravel() for a in arrays]), axis)]
    dot_general x35 -> x36, matrix products: 101 us -> 236 us  [ein(): return jnp.einsum(spec, a, b, precision=lax.Precision.HIGHEST)]
    all_to_all x23 -> x2, starting transfers between devices: 128 us -> 8.36 us  [the longest x1 4.48 us: local(): pair = lax.all_to_all(by_dest, ('zlo',) + BOND, 0, 0, tiled=True)]
    unnamed x104 -> x55, local copies, waits for them, and re-layouts: 117 us -> 7.98 us
    all_to_all x25 -> x0, local copies, waits for them, and re-layouts: 83.9 us -> none  [the longest x5 23.3 us: down_parts(): lax.all_to_all(side, 'node', split_axis=3, concat_axis=4, tiled=True)]
    all_to_all x23 -> x2, waiting for transfers between devices: 80.4 us -> 9.56 us  [the longest x1 9.56 us: local(): pieces = lax.all_to_all(pieces, BOND, 0, 0, tiled=True)]
    all_to_all x19 -> x0, other arithmetic: 46.1 us -> none  [the longest x4 11.1 us: down_parts(): lax.all_to_all(worked_all, 'bond', split_axis=2, concat_axis=4, tiled=True)]
    all_gather x1 -> x2, waiting for transfers between devices: 0.03 us -> 33.3 us  [the longest x1 33.3 us: local(): upper = lax.all_gather(shard, BOND, axis=0, tiled=True)]
  transfers between devices with their start and end apart: 29 -> 23, of which waited for: 18 -> 3; matrix products, arithmetic and copies ran while one was open for 19% -> 60% of each run, Pallas kernels for 0% -> 0%
where the time goes in v1:
time: 516 us; the launch traced here: 506 us
  matrix products  236 us (46%)
  local copies, waits for them, and re-layouts  108 us (21%)
  blocking collectives  68.9 us (13%)
  waiting for transfers between devices  43.7 us (8%)
  starting transfers between devices  32.5 us (6%)
  between operations  15.1 us (3%)
    dot_general x36, matrix products, ein(): return jnp.einsum(spec, a, b, precision=lax.Precision.HIGHEST)  236 us
    dot_general x9, local copies, waits for them, and re-layouts, ein(): return jnp.einsum(spec, a, b, precision=lax.Precision.HIGHEST)  51.9 us
    all_to_all x1, blocking collectives, local(): both = lax.all_to_all(both, BOND, 0, 0, tiled=True)  43.7 us
    all_gather x1, waiting for transfers between devices, local(): upper = lax.all_gather(shard, BOND, axis=0, tiled=True)  33.3 us
    dynamic_slice x3, local copies, waits for them, and re-layouts, halves(): return lax.dynamic_slice_in_dim(tensor, core * size, size, axis=axis)  21.2 us
    ppermute x13, starting transfers between devices, move(): return lax.ppermute(x, NODE, pairs)  19.7 us
    all_to_all x1, blocking collectives, local(): got = lax.all_to_all(send, NODE, 0, 0, tiled=True)  15.3 us
  transfers between devices with their start and end apart: 23, of which 3 were waited for; matrix products, arithmetic and copies ran while one was open for 60% of the time, Pallas kernels for 0%

profile of v1, /device:TPU:1, one launch (start us, length us, event | category | flops | bytes accessed | tf_op | source)
XLA Modules:
  0.0 506.0 jit_solution(13400908433034332693)
XLA Ops:
  14.1 15.3 %all_to_all.20 = f32[8,8,16,128]{3,2,1,0:T(8,128)S(1)} all-to-all(f32[8,8,16,128]{3,2,1,0:T(8,128)S(1)} %slice_dynamic-update-slice_fusion), channel_id=1, replica_groups=mesh['ylo'=2,'zhi'=2,'zlo'=2,'yhi'=2,'x'=4,'core'=2] {'ylo','zhi','zlo'}, dimensions={0} | all-to-all | bytes 1048576 | tf_op jit(solution)/shard_map/all_to_all | solution.py:47
  34.8 43.7 %all_to_all.21 = f32[16,4,8,8,128]{4,3,2,1,0:T(8,128)S(1)} all-to-all(f32[16,4,8,8,128]{4,3,2,1,0:T(8,128)S(1)} %copy_bitcast_fusion.2), channel_id=1, replica_groups=mesh['ylo'=2,'zhi'=2,'zlo'=2,'yhi'=2,'x'=4,'core'=2] {'yhi','x','core'}, dimensions={0} | all-to-all | bytes 4194304 | tf_op jit(solution)/shard_map/all_to_all | solution.py:58
  85.1 9.6 %all-to-all-done.2 = f32[16,3,8,128]{3,2,1,0:T(8,128)S(1)} async-done(((f32[16,3,8,128]{3,2,1,0:T(8,128)}), f32[16,3,8,128]{3,2,1,0:T(8,128)S(1)}, u32[]{:S(2)}, u32[]{:S(2)}) %all-to-all-start.2) | async-done | bytes 196640 | tf_op jit(solution)/shard_map/all_to_all | solution.py:63
  99.9 33.3 %all-gather.4.cloned.1.call-done = f32[128,128,128]{2,0,1:T(8,128)} async-done(((f32[8,128,128]{2,0,1:T(8,128)}), f32[128,128,128]{2,0,1:T(8,128)}) %all-gather.4.cloned.1.call-update) | async-done | bytes 8388624 | tf_op jit(solution)/shard_map/all_gather | solution.py:49
  138.2 8.7 %fusion.26 = f32[128,64,128]{2,0,1:T(8,128)S(1)} fusion(f32[64,128,128]{2,0,1:T(8,128)} %constant_dynamic-slice_fusion.1, f32[32,8,128]{2,1,0:T(8,128)S(1)} %all-to-all-done.3), kind=kOutput, calls=%fused_computation.26 | convolution fusion | flops 1610612736 | bytes 8454144 | tf_op jit(solution)/shard_map/pab,ac->pcb/dot_general | solution.py:12
  153.3 9.0 %convolution_bitcast_fusion.6 = f32[64,128]{1,0:T(8,128)S(1)} fusion(f32[64,128,128]{2,0,1:T(8,128)S(1)} %fusion.14, f32[128,128,128]{2,0,1:T(8,128)S(1)} %bitcast.242), kind=kOutput, calls=%fused_computation.59 | convolution fusion | flops 1610612736 | bytes 12615680 | tf_op jit(solution)/shard_map/pcd,qcd->pq/dot_general | solution.py:12
  177.6 9.4 %copy.46 = f32[128,128,128]{1,0,2:T(8,128)} copy(f32[128,128,128]{2,0,1:T(8,128)} %all-gather.4.cloned.1.call-done) | data formatting | bytes 16777216 | tf_op jit(solution)/shard_map/all_gather | solution.py:49
  187.0 10.9 %fusion.101 = f32[128,128,128]{1,0,2:T(8,128)S(1)} fusion(f32[128,128,128]{1,0,2:T(8,128)} %copy.46, f32[3,128,128]{2,1,0:T(8,128)S(1)} %copy-done, s32[]{:T(128)S(6)} %select_n.104), kind=kOutput, calls=%fused_computation.118 | convolution fusion | flops 3221225472 | bytes 16842756 | tf_op jit(solution)/shard_map/pq,qcd->pcd/dot_general | solution.py:12
  203.8 9.0 %constant_dynamic-slice_fusion = f32[128,128,64]{2,0,1:T(8,128)} fusion(f32[128,128,128]{2,0,1:T(8,128)} %all-gather.4.cloned.1.call-done, s32[]{:T(128)S(6)} %select_n.97), kind=kLoop, calls=%fused_computation.152 | loop fusion | bytes 8388612 | tf_op jit(solution)/shard_map/dynamic_slice | solution.py:34
  221.7 11.8 %fusion.92 = f32[128,128,128]{2,0,1:T(8,128)} fusion(f32[128,128,128]{2,0,1:T(8,128)} %all-gather.4.cloned.1.call-done, f32[64,128]{1,0:T(8,128)S(1)} %get-tuple-element.21, f32[64,128]{1,0:T(8,128)S(1)} %get-tuple-element.20), kind=kOutput, calls=%fused_computation.106 | convolution fusion | flops 3221241856 | bytes 16842752 | tf_op jit(solution)/shard_map/pq,qcd->pcd/dot_general | solution.py:12
  233.4 9.4 %copy.27 = f32[128,128,128]{1,0,2:T(8,128)} copy(f32[128,128,128]{2,0,1:T(8,128)} %fusion.92) | data formatting | bytes 16777216 | tf_op jit(solution)/shard_map/pq,qcd->pcd/dot_general | solution.py:12
  242.9 8.8 %fusion.24 = f32[128,64,128]{2,0,1:T(8,128)S(1)} fusion(f32[64,128,128]{2,0,1:T(8,128)} %constant_dynamic-slice_fusion.1, f32[2,64,128]{2,1,0:T(8,128)S(1)} %get-tuple-element.15, f32[2,64,128]{2,1,0:T(8,128)S(1)} %get-tuple-element.14), kind=kOutput, calls=%fused_computation.24 | convolution fusion | flops 1610629120 | bytes 8519680 | tf_op jit(solution)/shard_map/pab,ac->pcb/dot_general | solution.py:12
  258.0 9.2 %convolution_bitcast_fusion.5 = f32[64,128]{1,0:T(8,128)S(1)} fusion(f32[64,128,128]{2,0,1:T(8,128)S(1)} %fusion.12, f32[128,128,128]{2,0,1:T(8,128)S(1)} %bitcast.244), kind=kOutput, calls=%fused_computation.58 | convolution fusion | flops 1610612736 | bytes 12615680 | tf_op jit(solution)/shard_map/pcd,qcd->pq/dot_general | solution.py:12
  290.1 11.0 %fusion.45 = f32[64,128]{1,0:T(8,128)S(1)} fusion(f32[128,128,128]{2,0,1:T(8,128)} %fusion.92, f32[128,128,64]{1,0,2:T(8,128)S(1)} %fusion.111), kind=kOutput, calls=%fused_computation.47 | convolution fusion | flops 1610612736 | bytes 12615680 | tf_op jit(solution)/shard_map/pcb,pcd->bd/dot_general | solution.py:12
  312.2 8.3 %convolution_bitcast_fusion.3 = f32[64,128]{1,0:T(8,128)S(1)} fusion(f32[128,64,128]{0,1,2:T(8,128)} %copy.44, f32[128,128,128]{1,0,2:T(8,128)} %copy.27), kind=kOutput, calls=%fused_computation.56 | convolution fusion | flops 1610612736 | bytes 12615680 | tf_op jit(solution)/shard_map/pad,pcd->ac/dot_general | solution.py:12
  334.6 8.8 %fusion.54 = f32[64,128]{1,0:T(8,128)S(1)} fusion(f32[64,128,128]{2,0,1:T(8,128)S(1)} %fusion.4, f32[128,128,128]{2,0,1:T(8,128)S(1)} %bitcast.248, pred[]{:T(512)S(6)} %eq.9), kind=kOutput, calls=%fused_computation.51 | convolution fusion | flops 1610620928 | bytes 12615681 | tf_op jit(solution)/shard_map/pcd,qcd->pq/dot_general | solution.py:12
  344.9 9.5 %fusion.95 = f32[128,128,128]{2,0,1:T(8,128)} fusion(f32[128,128,128]{2,0,1:T(8,128)S(1)} %bitcast.248, f32[64,128]{1,0:T(8,128)S(1)} %get-tuple-element.19, f32[64,128]{1,0:T(8,128)S(1)} %get-tuple-element.18), kind=kOutput, calls=%fused_computation.110 | convolution fusion | flops 3221241856 | bytes 16842752 | tf_op jit(solution)/shard_map/pq,qcd->pcd/dot_general | solution.py:12
  354.4 9.4 %copy.28 = f32[128,128,128]{1,0,2:T(8,128)} copy(f32[128,128,128]{2,0,1:T(8,128)} %fusion.95) | data formatting | bytes 16777216 | tf_op jit(solution)/shard_map/pq,qcd->pcd/dot_general | solution.py:12
  363.8 10.7 %fusion.48 = f32[64,128]{1,0:T(8,128)S(1)} fusion(f32[128,128,128]{2,0,1:T(8,128)} %fusion.95, f32[128,128,64]{1,0,2:T(8,128)} %fusion.107), kind=kOutput, calls=%fused_computation.48 | convolution fusion | flops 1610612736 | bytes 12615680 | tf_op jit(solution)/shard_map/pcb,pcd->bd/dot_general | solution.py:12
  402.1 10.5 %fusion.98 = f32[128,128,128]{2,0,1:T(8,128)S(1)} fusion(f32[128,128,128]{2,0,1:T(8,128)} %all-gather.4.cloned.1.call-done, f32[64,128]{1,0:T(8,128)S(1)} %get-tuple-element.17, f32[64,128]{1,0:T(8,128)S(1)} %get-tuple-element.16), kind=kOutput, calls=%fused_computation.114 | convolution fusion | flops 3221241856 | bytes 16842752 | tf_op jit(solution)/shard_map/pq,qcd->pcd/dot_general | solution.py:12
  426.4 9.4 %copy.29 = f32[128,128,128]{1,0,2:T(8,128)} copy(f32[128,128,128]{2,0,1:T(8,128)} %copy-done.2) | data formatting | bytes 16777216 | tf_op jit(solution)/shard_map/pq,qcd->pcd/dot_general | solution.py:12
  435.8 8.2 %fusion.56 = f32[1,64,128]{2,1,0:T(8,128)S(1)} fusion(f32[64,128]{1,0:T(8,128)S(1)} %collective-permute-done.14, f32[128,64,128]{0,1,2:T(8,128)} %copy.39, f32[128,128,128]{1,0,2:T(8,128)} %copy.29, pred[]{:T(512)S(6)} %eq.8), kind=kOutput, calls=%fused_computation.54 | convolution fusion | flops 1610620928 | bytes 12648449 | tf_op jit(solution)/shard_map/pad,pcd->ac/dot_general | solution.py:12
  444.0 9.9 %all-gather = f32[8,64,128]{2,1,0:T(8,128)S(1)} all-gather(f32[2,64,128]{2,1,0:T(8,128)S(1)} %pad_maximum_fusion.5), channel_id=2, replica_groups=mesh['ylo'=2,'zhi'=2,'zlo'=2,'yhi'=2,'x'=4,'core'=2] {'x'}, dimensions={0}, use_global_device_ids=true | all-gather | bytes 327680 | tf_op jit(solution)/shard_map/all_gather | solution.py:124
  475.2 9.6 %copy.33 = f32[128,128,128]{2,0,1:T(8,128)} copy(f32[128,128,128]{1,0,2:T(8,128)} %all-gather.6.cloned.1.call-done) | data formatting | bytes 16777216 | tf_op jit(solution)/shard_map/all_gather | solution.py:129
  (167 shorter events, 197.7 us)
Async XLA Ops:
  7.2 179.8 %copy-start = (f32[3,128,128]{2,1,0:T(8,128)S(1)}, f32[3,128,128]{2,1,0:T(8,128)}, u32[]{:S(2)}) copy-start(f32[3,128,128]{2,1,0:T(8,128)} %param.9) | copy-start | bytes 589828
  7.2 126.1 %all-gather.4.cloned.1.call-start = ((), (), s32[]{:S(2)}) async-start(), calls=%async_computation.4 | async-start | bytes 8912896 | tf_op jit(solution)/shard_map/all_gather | solution.py:49
  81.2 13.4 %all-to-all-start.2 = ((f32[16,3,8,128]{3,2,1,0:T(8,128)}), f32[16,3,8,128]{3,2,1,0:T(8,128)S(1)}, u32[]{:S(2)}, u32[]{:S(2)}) async-start(f32[16,3,8,128]{3,2,1,0:T(8,128)} %bitcast.240), calls=%async_computation.2 | async-start | bytes 393216 | tf_op jit(solution)/shard_map/all_to_all | solution.py:63
  95.4 42.8 %all-to-all-start.3 = ((f32[32,8,128]{2,1,0:T(8,128)}), f32[32,8,128]{2,1,0:T(8,128)S(1)}, u32[]{:S(2)}, u32[]{:S(2)}) async-start(f32[32,8,128]{2,1,0:T(8,128)} %bitcast.22), calls=%async_computation.3 | async-start | bytes 262144 | tf_op jit(solution)/shard_map/all_to_all | solution.py:68
  99.9 366.5 %all-gather.6.cloned.1.call-start = ((), (), s32[]{:S(2)}) async-start(), calls=%async_computation.5 | async-start | bytes 8912896 | tf_op jit(solution)/shard_map/all_gather | solution.py:129
  162.2 58.6 %collective-permute-start = (f32[64,128]{1,0:T(8,128)S(1)}, f32[64,128]{1,0:T(8,128)S(1)}, u32[]{:S(2)}, u32[]{:S(2)}) collective-permute-start(f32[64,128]{1,0:T(8,128)S(1)} %convolution_bitcast_fusion.6), channel_id=1, source_target_pairs={{0,16},{64,80},{1,17},{65,81},{2,18},{66,82},{3,19},{67,83},{4,20}... | collective-permute-start | bytes 98312 | tf_op jit(solution)/shard_map/ppermute | solution.py:72
  165.8 55.0 %collective-permute-start.1 = (f32[64,128]{1,0:T(8,128)S(1)}, f32[64,128]{1,0:T(8,128)S(1)}, u32[]{:S(2)}, u32[]{:S(2)}) collective-permute-start(f32[64,128]{1,0:T(8,128)S(1)} %convolution_bitcast_fusion.6), channel_id=1, source_target_pairs={{32,16},{96,80},{33,17},{97,81},{34,18},{98,82},{35,19},{99,83},{3... | collective-permute-start | bytes 98312 | tf_op jit(solution)/shard_map/ppermute | solution.py:72
  203.2 17.0 %collective-permute-start.6 = (f32[64,128]{1,0:T(8,128)S(1)}, f32[64,128]{1,0:T(8,128)S(1)}, u32[]{:S(2)}, u32[]{:S(2)}) collective-permute-start(f32[64,128]{1,0:T(8,128)S(1)} %convolution_bitcast_fusion.4), channel_id=1, source_target_pairs={{112,48},{113,49},{114,50},{115,51},{116,52},{117,53},{118,54},{11... | collective-permute-start | bytes 98312 | tf_op jit(solution)/shard_map/ppermute | solution.py:72
  220.2 1.5 collective-permute-start.7
  220.8 22.0 %collective-permute-start.2 = (f32[2,64,128]{2,1,0:T(8,128)S(1)}, f32[2,64,128]{2,1,0:T(8,128)S(1)}, u32[]{:S(2)}, u32[]{:S(2)}) collective-permute-start(f32[2,64,128]{2,1,0:T(8,128)S(1)} %pad_maximum_fusion.3), channel_id=1, source_target_pairs={{0,1},{1,0},{2,3},{3,2},{4,5},{5,4},{6,7},{7,6},{8,9},{9,8},{10,11... | collective-permute-start | bytes 196616 | tf_op jit(solution)/shard_map/ppermute | solution.py:20
  267.2 6.5 %collective-permute-start.3 = (f32[64,128]{1,0:T(8,128)S(1)}, f32[64,128]{1,0:T(8,128)S(1)}, u32[]{:S(2)}, u32[]{:S(2)}) collective-permute-start(f32[64,128]{1,0:T(8,128)S(1)} %convolution_bitcast_fusion.5), channel_id=1, source_target_pairs={{16,48},{17,49},{18,50},{19,51},{20,52},{21,53},{22,54},{23,55},{2... | collective-permute-start | bytes 98312 | tf_op jit(solution)/shard_map/ppermute | solution.py:72
  267.9 5.8 %collective-permute-start.4 = (f32[64,128]{1,0:T(8,128)S(1)}, f32[64,128]{1,0:T(8,128)S(1)}, u32[]{:S(2)}, u32[]{:S(2)}) collective-permute-start(f32[64,128]{1,0:T(8,128)S(1)} %convolution_bitcast_fusion.5), channel_id=1, source_target_pairs={{80,48},{81,49},{82,50},{83,51},{84,52},{85,53},{86,54},{87,55},{8... | collective-permute-start | bytes 98312 | tf_op jit(solution)/shard_map/ppermute | solution.py:72
  273.8 10.7 %collective-permute-start.5 = (f32[2,64,128]{2,1,0:T(8,128)S(1)}, f32[2,64,128]{2,1,0:T(8,128)S(1)}, u32[]{:S(2)}, u32[]{:S(2)}) collective-permute-start(f32[2,64,128]{2,1,0:T(8,128)S(1)} %pad_maximum_fusion.4), channel_id=1, source_target_pairs={{0,1},{1,0},{2,3},{3,2},{4,5},{5,4},{6,7},{7,6},{8,9},{9,8},{10,11... | collective-permute-start | bytes 196616 | tf_op jit(solution)/shard_map/ppermute | solution.py:20
  301.1 33.2 %collective-permute-start.9 = (f32[64,128]{1,0:T(8,128)S(1)}, f32[64,128]{1,0:T(8,128)S(1)}, u32[]{:S(2)}, u32[]{:S(2)}) collective-permute-start(f32[64,128]{1,0:T(8,128)S(1)} %fusion.45), channel_id=1, source_target_pairs={{48,80},{49,81},{50,82},{51,83},{52,84},{53,85},{54,86},{55,87},{5... | collective-permute-start | bytes 98312 | tf_op jit(solution)/shard_map/ppermute | solution.py:72
  320.6 13.8 %collective-permute-start.8 = (f32[64,128]{1,0:T(8,128)S(1)}, f32[64,128]{1,0:T(8,128)S(1)}, u32[]{:S(2)}, u32[]{:S(2)}) collective-permute-start(f32[64,128]{1,0:T(8,128)S(1)} %convolution_bitcast_fusion.3), channel_id=1, source_target_pairs={{48,16},{49,17},{50,18},{51,19},{52,20},{53,21},{54,22},{55,23},{5... | collective-permute-start | bytes 98312 | tf_op jit(solution)/shard_map/ppermute | solution.py:72
  334.4 10.5 %collective-permute-start.10 = (f32[64,128]{1,0:T(8,128)S(1)}, f32[64,128]{1,0:T(8,128)S(1)}, u32[]{:S(2)}, u32[]{:S(2)}) collective-permute-start(f32[64,128]{1,0:T(8,128)S(1)} %add.49), channel_id=1, source_target_pairs={{0,1},{1,0},{2,3},{3,2},{4,5},{5,4},{6,7},{7,6},{8,9},{9,8},{10,11... | collective-permute-start | bytes 98312 | tf_op jit(solution)/shard_map/ppermute | solution.py:20
  343.4 45.7 %collective-permute-start.15 = (f32[64,128]{1,0:T(8,128)S(1)}, f32[64,128]{1,0:T(8,128)S(1)}, u32[]{:S(2)}, u32[]{:S(2)}) collective-permute-start(f32[64,128]{1,0:T(8,128)S(1)} %fusion.54), channel_id=1, source_target_pairs={{48,112},{49,113},{50,114},{51,115},{52,116},{53,117},{54,118},{55... | collective-permute-start | bytes 98312 | tf_op jit(solution)/shard_map/ppermute | solution.py:72
  374.5 15.4 %collective-permute-start.12 = (f32[64,128]{1,0:T(8,128)S(1)}, f32[64,128]{1,0:T(8,128)S(1)}, u32[]{:S(2)}, u32[]{:S(2)}) collective-permute-start(f32[64,128]{1,0:T(8,128)S(1)} %fusion.48), channel_id=1, source_target_pairs={{16,32},{80,96},{17,33},{81,97},{18,34},{82,98},{19,35},{83,99},{2... | collective-permute-start | bytes 98312 | tf_op jit(solution)/shard_map/ppermute | solution.py:72
  382.6 7.2 %collective-permute-start.11 = (f32[64,128]{1,0:T(8,128)S(1)}, f32[64,128]{1,0:T(8,128)S(1)}, u32[]{:S(2)}, u32[]{:S(2)}) collective-permute-start(f32[64,128]{1,0:T(8,128)S(1)} %convolution_bitcast_fusion.2), channel_id=1, source_target_pairs={{16,0},{80,64},{17,1},{81,65},{18,2},{82,66},{19,3},{83,67},{20,4}... | collective-permute-start | bytes 98312 | tf_op jit(solution)/shard_map/ppermute | solution.py:72
  389.1 11.3 %collective-permute-start.16 = (f32[64,128]{1,0:T(8,128)S(1)}, f32[64,128]{1,0:T(8,128)S(1)}, u32[]{:S(2)}, u32[]{:S(2)}) collective-permute-start(f32[64,128]{1,0:T(8,128)S(1)} %add.51), channel_id=1, source_target_pairs={{48,16},{112,80},{49,17},{113,81},{50,18},{114,82},{51,19},{115,83... | collective-permute-start | bytes 98312 | tf_op jit(solution)/shard_map/ppermute | solution.py:72
  389.8 12.3 %collective-permute-start.13 = (f32[64,128]{1,0:T(8,128)S(1)}, f32[64,128]{1,0:T(8,128)S(1)}, u32[]{:S(2)}, u32[]{:S(2)}) collective-permute-start(f32[64,128]{1,0:T(8,128)S(1)} %add.50), channel_id=1, source_target_pairs={{0,1},{1,0},{2,3},{3,2},{4,5},{5,4},{6,7},{7,6},{8,9},{9,8},{10,11... | collective-permute-start | bytes 98312 | tf_op jit(solution)/shard_map/ppermute | solution.py:20
  400.4 25.9 %collective-permute-start.17 = (f32[64,128]{1,0:T(8,128)S(1)}, f32[64,128]{1,0:T(8,128)S(1)}, u32[]{:S(2)}, u32[]{:S(2)}) collective-permute-start(f32[64,128]{1,0:T(8,128)S(1)} %add.52), channel_id=1, source_target_pairs={{48,32},{16,0},{112,96},{80,64},{49,33},{17,1},{113,97},{81,65},{5... | collective-permute-start | bytes 98312 | tf_op jit(solution)/shard_map/ppermute | solution.py:72
  420.1 15.7 %collective-permute-start.14 = (f32[64,128]{1,0:T(8,128)S(1)}, f32[64,128]{1,0:T(8,128)S(1)}, u32[]{:S(2)}, u32[]{:S(2)}) collective-permute-start(f32[64,128]{1,0:T(8,128)S(1)} %fusion.51), channel_id=1, source_target_pairs={{0,16},{32,48},{64,80},{96,112},{1,17},{33,49},{65,81},{97,113},{2... | collective-permute-start | bytes 98312 | tf_op jit(solution)/shard_map/ppermute | solution.py:72
  453.9 7.7 %collective-permute-start.18 = (f32[3,2,64,128]{3,2,0,1:T(8,128)S(1)}, f32[3,2,64,128]{3,2,0,1:T(8,128)S(1)}, u32[]{:S(2)}, u32[]{:S(2)}) collective-permute-start(f32[3,2,64,128]{3,2,0,1:T(8,128)S(1)} %copy.31), channel_id=1, source_target_pairs={{0,1},{1,0},{2,3},{3,2},{4,5},{5,4},{6,7},{7,6},{8,9},{9,8},{10,11... | collective-permute-start | bytes 589832 | tf_op jit(solution)/shard_map/ppermute | solution.py:20
  (22 other events, 257.6 us)
Sparse Core Ops, SparseCore 0:
  30.5 102.7 all-gather.3
  135.5 76.0 all-gather.5
